TPU v7x, 32 devices: a whole 2x2x4 slice. The times are simulated.
32 devices in a mesh: layer: 2 (over core), prow: 4 (over z), pcol: 4 (over y, x).
Axes of the slice: x: 2, y: 2, z: 4, core: 2. Of those that a mesh axis runs over, the one named last changes fastest.
Arguments:
- diag_inverse: float32 [2, 3, 2048, 2048], P('layer', None, 'prow', 'pcol'), may hold values from -1 to 1, as said below
- root_inverse: float32 [2048, 2048], P('prow', 'pcol'), may hold values from -1 to 1, as said below
- coupling: float32 [2, 5, 2048, 2048], P('layer', None, 'prow', 'pcol'), may hold values from -0.0625 to 0.0625
- tile_mask: int32 [2, 5, 16, 16], P('layer'), may hold values 0 or 1
- sketch: float32 [2, 3, 2048, 256], P('layer', None, 'prow'), may hold values from -6 to 6
- root_sketch: float32 [2048, 256], P('prow'), may hold values from -6 to 6
Outputs:
- solution: float32 [2, 3, 2048, 256], P('layer', None, 'prow')
- root_solution: float32 [2048, 256], P('prow')
Inputs may be any that keep to these rules, and one draw needn't show every extreme that they name: `diag_inverse`: lower triangular. `root_inverse`: lower triangular.
All inputs are finite; a program needn't handle non-finite values. No bound on the sum of `tile_mask` on one device may be relied on, other than what follows from the above.
Results may differ from a plain program's by a relative error of at most 0.0001.
Values sent between devices are 32-bit elements; how exact they have to be, the bound alone decides.
No kernel may reach another device: no remote copies, remote signals or barrier semaphores. Data moves between devices by JAX's collectives and lax.ppermute only.
A program may use at most 64 MiB of HBM per device.

v0:
```python
import jax
import jax.numpy as jnp
from jax import lax
from jax.sharding import PartitionSpec as P

TILE = 128


def broadcast(block, axis, owner):
    block = jnp.where(lax.axis_index(axis) == owner, block, jnp.zeros_like(block))
    return lax.psum(block, axis)


def forward_product(matrix, vector):
    return jnp.einsum("nij,njk->nik", matrix, vector, precision=lax.Precision.HIGHEST)


def transpose_product(matrix, vector):
    return jnp.einsum("nij,nik->njk", matrix, vector, precision=lax.Precision.HIGHEST)


def column_panel(vector):
    group_ratio = lax.axis_size("pcol") // lax.axis_size("prow")
    col_index = lax.axis_index("pcol")
    received = broadcast(vector, "prow", col_index // group_ratio)
    col_width = vector.shape[1] // group_ratio
    return lax.dynamic_slice_in_dim(received, col_index % group_ratio * col_width, col_width, 1)


def column_total(partial_value):
    return lax.psum(partial_value, "pcol")


def regroup(column_rows):
    group_ratio = lax.axis_size("pcol") // lax.axis_size("prow")
    row_index = lax.axis_index("prow")
    col_width = column_rows.shape[1]
    complete = lax.all_gather(column_rows, "pcol", axis=1, tiled=True)
    return lax.dynamic_slice_in_dim(
        complete, row_index * (col_width * group_ratio), col_width * group_ratio, 1
    )


def row_total(partial_value):
    return regroup(lax.psum(partial_value, "prow"))


def local_mask(tile_mask, rows_here, cols_here):
    row_tiles = (lax.axis_index("prow") * rows_here + lax.iota(jnp.int32, rows_here)) // TILE
    col_tiles = (lax.axis_index("pcol") * cols_here + lax.iota(jnp.int32, cols_here)) // TILE
    table = jnp.take(tile_mask[0], row_tiles, axis=1)
    table = jnp.take(table, col_tiles, axis=2)
    return table.astype(jnp.float32)


def per_device(diag_inverse, root_inverse, coupling, tile_mask, sketch, root_sketch):
    layer_inverse = diag_inverse[0]
    rows_here = coupling.shape[2]
    cols_here = coupling.shape[3]
    blocks = coupling[0] * local_mask(tile_mask, rows_here, cols_here)
    rhs_local = sketch[0]
    leaves = column_total(forward_product(layer_inverse[0:2], column_panel(rhs_local[0:2])))
    fed_leaves = column_panel(leaves)
    mid_part = forward_product(blocks[0:2], fed_leaves)
    root_part = forward_product(blocks[2:4], fed_leaves)
    mid_rhs = rhs_local[2] - column_total(mid_part[0] + mid_part[1])
    middle = column_total(forward_product(layer_inverse[2:3], column_panel(mid_rhs[None])))[0]
    upper_part = forward_product(blocks[4:5], column_panel(middle[None]))[0]
    update = lax.psum(root_part[0] + root_part[1] + upper_part, ("layer", "pcol"))
    root_forward = column_total(
        forward_product(root_inverse[None], column_panel((root_sketch - update)[None]))
    )[0]
    root_solution = row_total(transpose_product(root_inverse[None], root_forward[None]))[0]
    spread_root = jnp.broadcast_to(root_solution, (3,) + root_solution.shape)
    back_terms = row_total(transpose_product(blocks[2:5], spread_root))
    mid_back = middle - back_terms[2]
    mid_solution = row_total(transpose_product(layer_inverse[2:3], mid_back[None]))[0]
    spread_mid = jnp.broadcast_to(mid_solution, (2,) + mid_solution.shape)
    leaf_terms = row_total(transpose_product(blocks[0:2], spread_mid))
    leaf_back = leaves - leaf_terms - back_terms[0:2]
    leaf_solution = row_total(transpose_product(layer_inverse[0:2], leaf_back))
    solution = jnp.concatenate([leaf_solution, mid_solution[None]], axis=0)[None]
    return (solution, root_solution)


def solution(mesh):
    in_specs = (
        P("layer", None, "prow", "pcol"),
        P("prow", "pcol"),
        P("layer", None, "prow", "pcol"),
        P("layer", None, None, None),
        P("layer", None, "prow", None),
        P("prow", None),
    )
    out_specs = (P("layer", None, "prow", None), P("prow", None))
    return jax.shard_map(
        per_device, mesh=mesh, in_specs=in_specs, out_specs=out_specs, check_vma=False
    )
```

profile of v0, /device:TPU:0, one launch (start us, length us, event | category | flops | bytes accessed | tf_op | source)
XLA Modules:
  0.0 1045.1 jit_solution(8067346142498596732)
XLA Ops:
  10.1 55.4 %all-reduce.16.cloned.1.call-done = f32[2,512,256]{1,2,0:T(8,128)} async-done(((f32[2,512,256]{1,2,0:T(8,128)}), f32[2,512,256]{1,2,0:T(8,128)}) %all-reduce.16.cloned.1.call-update) | async-done | bytes 1048592 | tf_op jit(solution)/shard_map/psum | solution.py:11
  65.5 4.8 fusion.6
  73.2 49.2 %all-reduce.18.cloned.1.call-done = f32[2,512,256]{1,2,0:T(8,128)} async-done(((f32[2,512,256]{1,2,0:T(8,128)}), f32[2,512,256]{1,2,0:T(8,128)}) %all-reduce.18.cloned.1.call-update) | async-done | bytes 1048592 | tf_op jit(solution)/shard_map/psum | solution.py:31
  124.8 3.4 select_bitcast_fusion
  129.0 4.4 gather_fusion.1
  133.4 8.8 copy.17
  142.2 7.9 bitcast_multiply_fusion
  150.1 27.3 %all-reduce.20.cloned.1.call-done = f32[2,512,256]{1,2,0:T(8,128)} async-done(((f32[2,512,256]{1,2,0:T(8,128)}), f32[2,512,256]{1,2,0:T(8,128)}) %all-reduce.20.cloned.1.call-update) | async-done | bytes 1048592 | tf_op jit(solution)/shard_map/psum | solution.py:11
  177.4 3.8 fusion.35
  182.2 44.8 %all-reduce.22.cloned.1.call-done = f32[512,256]{1,0:T(8,128)} async-done(((f32[512,256]{1,0:T(8,128)}), f32[512,256]{1,0:T(8,128)}) %all-reduce.22.cloned.1.call-update) | async-done | bytes 524304 | tf_op jit(solution)/shard_map/psum | solution.py:31
  229.1 39.0 %all-reduce.24.cloned.1.call-done = f32[512,256]{1,0:T(8,128)} async-done(((f32[512,256]{1,0:T(8,128)}), f32[512,256]{1,0:T(8,128)}) %all-reduce.24.cloned.1.call-update) | async-done | bytes 524304 | tf_op jit(solution)/shard_map/psum | solution.py:11
  268.1 4.0 convolution_bitcast_fusion.3
  272.2 45.4 %all-reduce.26.cloned.1.call-done = f32[1,512,256]{1,2,0:T(8,128)} async-done(((f32[1,512,256]{1,2,0:T(8,128)}), f32[1,512,256]{1,2,0:T(8,128)}) %all-reduce.26.cloned.1.call-update) | async-done | bytes 524304 | tf_op jit(solution)/shard_map/psum | solution.py:31
  319.8 3.6 fusion.36
  323.4 35.5 %all-reduce.28.cloned.1.call-done = f32[512,256]{0,1:T(8,128)} async-done(((f32[512,256]{0,1:T(8,128)}), f32[512,256]{0,1:T(8,128)}) %all-reduce.28.cloned.1.call-update) | async-done | bytes 524304 | tf_op jit(solution)/shard_map/psum | solution.py:11
  362.1 55.0 %all-reduce.30.cloned.1.call-done = f32[512,256]{1,0:T(8,128)} async-done(((f32[512,256]{1,0:T(8,128)}), f32[512,256]{1,0:T(8,128)}) %all-reduce.30.cloned.1.call-update) | async-done | bytes 524304 | tf_op jit(solution)/shard_map/psum | solution.py:69
  419.1 38.7 %all-reduce.32.cloned.1.call-done = f32[512,256]{1,0:T(8,128)} async-done(((f32[512,256]{1,0:T(8,128)}), f32[512,256]{1,0:T(8,128)}) %all-reduce.32.cloned.1.call-update) | async-done | bytes 524304 | tf_op jit(solution)/shard_map/psum | solution.py:11
  457.8 3.7 convolution_bitcast_fusion.2
  461.6 45.4 %all-reduce.34.cloned.1.call-done = f32[512,256]{0,1:T(8,128)} async-done(((f32[512,256]{0,1:T(8,128)}), f32[512,256]{0,1:T(8,128)}) %all-reduce.34.cloned.1.call-update) | async-done | bytes 524304 | tf_op jit(solution)/shard_map/psum | solution.py:31
  510.0 38.4 %all-reduce.36.cloned.1.call-done = f32[1,512,256]{1,2,0:T(8,128)} async-done(((f32[1,512,256]{1,2,0:T(8,128)}), f32[1,512,256]{1,2,0:T(8,128)}) %all-reduce.36.cloned.1.call-update) | async-done | bytes 524304 | tf_op jit(solution)/shard_map/psum | solution.py:45
  548.5 37.1 %all-gather.6.cloned.1.call-done = f32[1,2048,256]{1,2,0:T(8,128)} async-done(((f32[1,512,256]{1,2,0:T(8,128)}), f32[1,2048,256]{1,2,0:T(8,128)}) %all-gather.6.cloned.1.call-update) | async-done | bytes 2097168 | tf_op jit(solution)/shard_map/all_gather | solution.py:38
  586.9 6.1 fusion.18
  593.1 69.2 %all-reduce.38.cloned.1.call-done = f32[3,512,256]{1,2,0:T(8,128)} async-done(((f32[3,512,256]{1,2,0:T(8,128)}), f32[3,512,256]{1,2,0:T(8,128)}) %all-reduce.38.cloned.1.call-update) | async-done | bytes 1572880 | tf_op jit(solution)/shard_map/psum | solution.py:45
  662.4 71.0 %all-gather.8.cloned.1.call-done = f32[3,2048,256]{1,2,0:T(8,128)} async-done(((f32[3,512,256]{1,2,0:T(8,128)}), f32[3,2048,256]{1,2,0:T(8,128)}) %all-gather.8.cloned.1.call-update) | async-done | bytes 6291472 | tf_op jit(solution)/shard_map/all_gather | solution.py:38
  736.7 38.4 %all-reduce.40.cloned.1.call-done = f32[1,512,256]{1,2,0:T(8,128)} async-done(((f32[1,512,256]{1,2,0:T(8,128)}), f32[1,512,256]{1,2,0:T(8,128)}) %all-reduce.40.cloned.1.call-update) | async-done | bytes 524304 | tf_op jit(solution)/shard_map/psum | solution.py:45
  775.4 36.9 %all-gather.10.cloned.1.call-done = f32[1,2048,256]{1,2,0:T(8,128)} async-done(((f32[1,512,256]{1,2,0:T(8,128)}), f32[1,2048,256]{1,2,0:T(8,128)}) %all-gather.10.cloned.1.call-update) | async-done | bytes 2097168 | tf_op jit(solution)/shard_map/all_gather | solution.py:38
  813.6 4.7 fusion.25
  818.3 51.9 %all-reduce.42.cloned.1.call-done = f32[2,512,256]{1,2,0:T(8,128)} async-done(((f32[2,512,256]{1,2,0:T(8,128)}), f32[2,512,256]{1,2,0:T(8,128)}) %all-reduce.42.cloned.1.call-update) | async-done | bytes 1048592 | tf_op jit(solution)/shard_map/psum | solution.py:45
  870.3 53.8 %all-gather.12.cloned.1.call-done = f32[2,2048,256]{1,2,0:T(8,128)} async-done(((f32[2,512,256]{1,2,0:T(8,128)}), f32[2,2048,256]{1,2,0:T(8,128)}) %all-gather.12.cloned.1.call-update) | async-done | bytes 4194320 | tf_op jit(solution)/shard_map/all_gather | solution.py:38
  924.1 5.2 fusion.9
  929.3 51.9 %all-reduce.44.cloned.1.call-done = f32[2,512,256]{1,2,0:T(8,128)} async-done(((f32[2,512,256]{1,2,0:T(8,128)}), f32[2,512,256]{1,2,0:T(8,128)}) %all-reduce.44.cloned.1.call-update) | async-done | bytes 1048592 | tf_op jit(solution)/shard_map/psum | solution.py:45
  981.3 53.9 %all-gather.14.cloned.1.call-done = f32[2,2048,256]{1,2,0:T(8,128)} async-done(((f32[2,512,256]{1,2,0:T(8,128)}), f32[2,2048,256]{1,2,0:T(8,128)}) %all-gather.14.cloned.1.call-update) | async-done | bytes 4194320 | tf_op jit(solution)/shard_map/all_gather | solution.py:38
  (80 shorter events, 31.7 us)
Async XLA Ops:
  7.2 450.6 %copy-start = (f32[512,512]{1,0:T(8,128)S(1)}, f32[512,512]{1,0:T(8,128)}, u32[]{:S(2)}) copy-start(f32[512,512]{1,0:T(8,128)} %param.7) | copy-start | bytes 3145732
  7.2 58.3 %all-reduce.16.cloned.1.call-start = ((), (), s32[]{:S(2)}) async-start(), calls=%async_computation | async-start | bytes 2097152 | tf_op jit(solution)/shard_map/psum | solution.py:11
  10.0 60.4 %copy-start.6 = (s32[1,5,16,16]{3,2,1,0:T(8,128)S(1)}, s32[1,5,16,16]{3,2,1,0:T(8,128)}, u32[]{:S(2)}) copy-start(s32[1,5,16,16]{3,2,1,0:T(8,128)} %param.9) | copy-start | bytes 15364
  10.0 112.4 %all-reduce.18.cloned.1.call-start = ((), (), s32[]{:S(2)}) async-start(), calls=%async_computation.1 | async-start | bytes 2097152 | tf_op jit(solution)/shard_map/psum | solution.py:31
  70.4 107.0 %all-reduce.20.cloned.1.call-start = ((), (), s32[]{:S(2)}) async-start(), calls=%async_computation.2 | async-start | bytes 2097152 | tf_op jit(solution)/shard_map/psum | solution.py:11
  124.8 102.2 %all-reduce.22.cloned.1.call-start = ((), (), s32[]{:S(2)}) async-start(), calls=%async_computation.3 | async-start | bytes 1048576 | tf_op jit(solution)/shard_map/psum | solution.py:31
  182.1 137.7 %copy-start.2 = (f32[2,512,256]{1,2,0:T(8,128)S(1)}, f32[2,512,256]{1,2,0:T(8,128)}, u32[]{:S(2)}) copy-start(f32[2,512,256]{1,2,0:T(8,128)} %all-reduce.20.cloned.1.call-done) | copy-start | bytes 3145732
  182.1 86.0 %all-reduce.24.cloned.1.call-start = ((), (), s32[]{:S(2)}) async-start(), calls=%async_computation.4 | async-start | bytes 1048576 | tf_op jit(solution)/shard_map/psum | solution.py:11
  229.0 88.6 %all-reduce.26.cloned.1.call-start = ((), (), s32[]{:S(2)}) async-start(), calls=%async_computation.5 | async-start | bytes 1048576 | tf_op jit(solution)/shard_map/psum | solution.py:31
  272.1 86.7 %all-reduce.28.cloned.1.call-start = ((), (), s32[]{:S(2)}) async-start(), calls=%async_computation.6 | async-start | bytes 1048576 | tf_op jit(solution)/shard_map/psum | solution.py:11
  319.5 97.6 %all-reduce.30.cloned.1.call-start = ((), (), s32[]{:S(2)}) async-start(), calls=%async_computation.7 | async-start | bytes 1048576 | tf_op jit(solution)/shard_map/psum | solution.py:69
  323.3 93.8 %copy-start.5 = (f32[512,256]{1,0:T(8,128)S(1)}, f32[512,256]{1,0:T(8,128)}, u32[]{:S(2)}) copy-start(f32[512,256]{1,0:T(8,128)} %param.11) | copy-start | bytes 1572868
  362.1 95.7 %all-reduce.32.cloned.1.call-start = ((), (), s32[]{:S(2)}) async-start(), calls=%async_computation.8 | async-start | bytes 1048576 | tf_op jit(solution)/shard_map/psum | solution.py:11
  419.1 88.0 %all-reduce.34.cloned.1.call-start = ((), (), s32[]{:S(2)}) async-start(), calls=%async_computation.9 | async-start | bytes 1048576 | tf_op jit(solution)/shard_map/psum | solution.py:31
  461.5 86.9 %all-reduce.36.cloned.1.call-start = ((), (), s32[]{:S(2)}) async-start(), calls=%async_computation.10 | async-start | bytes 1048576 | tf_op jit(solution)/shard_map/psum | solution.py:45
  509.9 75.6 %all-gather.6.cloned.1.call-start = ((), (), s32[]{:S(2)}) async-start(), calls=%async_computation.11 | async-start | bytes 2621440 | tf_op jit(solution)/shard_map/all_gather | solution.py:38
  548.4 113.9 %all-reduce.38.cloned.1.call-start = ((), (), s32[]{:S(2)}) async-start(), calls=%async_computation.12 | async-start | bytes 3145728 | tf_op jit(solution)/shard_map/psum | solution.py:45
  586.9 6.2 copy-start.3
  593.0 140.4 %copy-start.4 = (f32[1,512,256]{1,2,0:T(8,128)S(1)}, f32[1,512,256]{1,2,0:T(8,128)}, u32[]{:S(2)}) copy-start(f32[1,512,256]{1,2,0:T(8,128)} %all-reduce.26.cloned.1.call-done) | copy-start | bytes 1572868
  593.0 140.3 %all-gather.8.cloned.1.call-start = ((), (), s32[]{:S(2)}) async-start(), calls=%async_computation.13 | async-start | bytes 7864320 | tf_op jit(solution)/shard_map/all_gather | solution.py:38
  662.3 112.8 %all-reduce.40.cloned.1.call-start = ((), (), s32[]{:S(2)}) async-start(), calls=%async_computation.14 | async-start | bytes 1048576 | tf_op jit(solution)/shard_map/psum | solution.py:45
  736.7 75.6 %all-gather.10.cloned.1.call-start = ((), (), s32[]{:S(2)}) async-start(), calls=%async_computation.15 | async-start | bytes 2621440 | tf_op jit(solution)/shard_map/all_gather | solution.py:38
  775.1 95.1 %all-reduce.42.cloned.1.call-start = ((), (), s32[]{:S(2)}) async-start(), calls=%async_computation.16 | async-start | bytes 2097152 | tf_op jit(solution)/shard_map/psum | solution.py:45
  813.6 110.5 %copy-start.1 = (f32[2,512,256]{1,2,0:T(8,128)S(1)}, f32[2,512,256]{1,2,0:T(8,128)}, u32[]{:S(2)}) copy-start(f32[2,512,256]{1,2,0:T(8,128)} %all-reduce.18.cloned.1.call-done) | copy-start | bytes 3145732
  818.3 105.8 %all-gather.12.cloned.1.call-start = ((), (), s32[]{:S(2)}) async-start(), calls=%async_computation.17 | async-start | bytes 5242880 | tf_op jit(solution)/shard_map/all_gather | solution.py:38
  870.3 111.0 %all-reduce.44.cloned.1.call-start = ((), (), s32[]{:S(2)}) async-start(), calls=%async_computation.18 | async-start | bytes 2097152 | tf_op jit(solution)/shard_map/psum | solution.py:45
  929.3 105.9 %all-gather.14.cloned.1.call-start = ((), (), s32[]{:S(2)}) async-start(), calls=%async_computation.19 | async-start | bytes 5242880 | tf_op jit(solution)/shard_map/all_gather | solution.py:38
Sparse Core Ops, SparseCore 0:
  11.0 54.5 all-reduce.15
  70.5 51.9 all-reduce.17
  125.5 51.8 all-reduce.19
  182.2 44.6 all-reduce.21
  229.7 38.2 all-reduce.23
  272.3 45.3 all-reduce.25
  320.5 38.2 all-reduce.27
  362.5 54.5 all-reduce.29
  420.2 37.5 all-reduce.31
  461.6 45.3 all-reduce.33
  510.1 38.2 all-reduce.35
  550.2 35.2 all-gather.5
  593.2 69.0 all-reduce.37
  664.1 69.1 all-gather.7
  736.8 38.2 all-reduce.39
  777.0 35.2 all-gather.9
  818.4 51.8 all-reduce.41
  872.0 52.0 all-gather.11
  929.4 51.8 all-reduce.43
  983.1 52.0 all-gather.13
where the time goes:
time: 1050 us
  waiting for transfers between devices  939 us (89%)
  matrix products  45.3 us (4%)
  local copies, waits for them, and re-layouts  23.8 us (2%)
  other arithmetic  21.5 us (2%)
  between operations  14.5 us (1%)
    all_gather x5, waiting for transfers between devices, regroup(): complete = lax.all_gather(column_rows, 'pcol', axis=1, tiled=True)  253 us
    psum x5, waiting for transfers between devices, row_total(): return regroup(lax.psum(partial_value, 'prow'))  250 us
    psum x5, waiting for transfers between devices, broadcast(): return lax.psum(block, axis)  196 us
    psum x4, waiting for transfers between devices, column_total(): return lax.psum(partial_value, 'pcol')  185 us
    psum x1, waiting for transfers between devices, per_device(): lax.psum(root_part[0] + root_part[1] + upper_part, ('layer', 'pcol'))  55 us
    dot_general x6, matrix products, forward_product(): jnp.einsum('nij,njk->nik', matrix, vector, precision=lax.Precision.HIGHEST)  23.2 us
    dot_general x5, matrix products, transpose_product(): jnp.einsum('nij,nik->njk', matrix, vector, precision=lax.Precision.HIGHEST)  22.1 us
  transfers between devices with their start and end apart: 20, of which 20 were waited for; matrix products, arithmetic and copies ran while one was open for 3% of the time, Pallas kernels for 0%

commit v1 on v0

--- a/solution.py
+++ b/solution.py
@@ -35,7 +35,27 @@
     group_ratio = lax.axis_size("pcol") // lax.axis_size("prow")
     row_index = lax.axis_index("prow")
     col_width = column_rows.shape[1]
-    complete = lax.all_gather(column_rows, "pcol", axis=1, tiled=True)
+    p_next = jax.lax.axis_size("pcol")
+    taken_in = jax.lax.axis_index("pcol")
+    r_now, local_next, high = (p_next, taken_in, column_rows.shape[1])
+    items = [(c, (c + 1) % r_now) for c in range(r_now)]
+    slots = [(c, (c - 1) % r_now) for c in range(r_now)]
+    complete = jnp.zeros(
+        (*column_rows.shape[:1], r_now * high, *column_rows.shape[2:]), column_rows.dtype
+    )
+    complete = lax.dynamic_update_slice_in_dim(complete, column_rows, local_next * high, axis=1)
+    value_now = earlier = column_rows
+    a_next = r_now // 2
+    for nth in [*range(1, a_next + 1)]:
+        value_now = jax.lax.ppermute(value_now, "pcol", items)
+        complete = lax.dynamic_update_slice_in_dim(
+            complete, value_now, (local_next - nth) % r_now * high, axis=1
+        )
+        if nth < r_now - a_next:
+            earlier = jax.lax.ppermute(earlier, "pcol", slots)
+            complete = lax.dynamic_update_slice_in_dim(
+                complete, earlier, (local_next + nth) % r_now * high, axis=1
+            )
     return lax.dynamic_slice_in_dim(
         complete, row_index * (col_width * group_ratio), col_width * group_ratio, 1
     )

time: 1050 us -> 1110 us (1.057)
  waiting for transfers between devices: 939 us -> 974 us
  starting transfers between devices: 1.22 us -> 18.3 us
    ppermute x0 -> x15, waiting for transfers between devices: none -> 292 us  [the longest x10 201 us: regroup(): value_now = jax.lax.ppermute(value_now, 'pcol', items)]
    all_gather x5 -> x0, waiting for transfers between devices: 253 us -> none  [regroup(): complete = lax.all_gather(column_rows, 'pcol', axis=1, tiled=True)]
    ppermute x0 -> x15, starting transfers between devices: none -> 17.5 us  [the longest x10 10.2 us: regroup(): value_now = jax.lax.ppermute(value_now, 'pcol', items)]
  transfers between devices with their start and end apart: 20 -> 30, of which waited for: 20 -> 30; matrix products, arithmetic and copies ran while one was open for 3% -> 4% of each run, Pallas kernels for 0% -> 0%
where the time goes in v1:
time: 1110 us
  waiting for transfers between devices  974 us (88%)
  matrix products  44.1 us (4%)
  local copies, waits for them, and re-layouts  33.4 us (3%)
  other arithmetic  21.7 us (2%)
  starting transfers between devices  18.3 us (2%)
  between operations  14.4 us (1%)
    psum x5, waiting for transfers between devices, row_total(): return regroup(lax.psum(partial_value, 'prow'))  245 us
    ppermute x10, waiting for transfers between devices, regroup(): value_now = jax.lax.ppermute(value_now, 'pcol', items)  201 us
    psum x5, waiting for transfers between devices, broadcast(): return lax.psum(block, axis)  196 us
    psum x4, waiting for transfers between devices, column_total(): return lax.psum(partial_value, 'pcol')  185 us
    ppermute x5, waiting for transfers between devices, regroup(): earlier = jax.lax.ppermute(earlier, 'pcol', slots)  91.6 us
    psum x1, waiting for transfers between devices, per_device(): lax.psum(root_part[0] + root_part[1] + upper_part, ('layer', 'pcol'))  55 us
    dot_general x6, matrix products, forward_product(): jnp.einsum('nij,njk->nik', matrix, vector, precision=lax.Precision.HIGHEST)  23.2 us
  transfers between devices with their start and end apart: 30, of which 30 were waited for; matrix products, arithmetic and copies ran while one was open for 4% of the time, Pallas kernels for 0%

profile of v1, /device:TPU:0, one launch (start us, length us, event | category | flops | bytes accessed | tf_op | source)
XLA Modules:
  0.0 1105.4 jit_solution(3638670156169952454)
XLA Ops:
  10.1 55.4 %all-reduce.16.cloned.1.call-done = f32[2,512,256]{1,2,0:T(8,128)} async-done(((f32[2,512,256]{1,2,0:T(8,128)}), f32[2,512,256]{1,2,0:T(8,128)}) %all-reduce.16.cloned.1.call-update) | async-done | bytes 1048592 | tf_op jit(solution)/shard_map/psum | solution.py:11
  73.2 49.2 %all-reduce.18.cloned.1.call-done = f32[2,512,256]{1,2,0:T(8,128)} async-done(((f32[2,512,256]{1,2,0:T(8,128)}), f32[2,512,256]{1,2,0:T(8,128)}) %all-reduce.18.cloned.1.call-update) | async-done | bytes 1048592 | tf_op jit(solution)/shard_map/psum | solution.py:31
  133.4 8.7 copy.19
  142.2 7.9 bitcast_multiply_fusion
  150.1 27.3 %all-reduce.20.cloned.1.call-done = f32[2,512,256]{1,2,0:T(8,128)} async-done(((f32[2,512,256]{1,2,0:T(8,128)}), f32[2,512,256]{1,2,0:T(8,128)}) %all-reduce.20.cloned.1.call-update) | async-done | bytes 1048592 | tf_op jit(solution)/shard_map/psum | solution.py:11
  182.2 44.8 %all-reduce.22.cloned.1.call-done = f32[512,256]{1,0:T(8,128)} async-done(((f32[512,256]{1,0:T(8,128)}), f32[512,256]{1,0:T(8,128)}) %all-reduce.22.cloned.1.call-update) | async-done | bytes 524304 | tf_op jit(solution)/shard_map/psum | solution.py:31
  229.1 39.0 %all-reduce.24.cloned.1.call-done = f32[512,256]{1,0:T(8,128)} async-done(((f32[512,256]{1,0:T(8,128)}), f32[512,256]{1,0:T(8,128)}) %all-reduce.24.cloned.1.call-update) | async-done | bytes 524304 | tf_op jit(solution)/shard_map/psum | solution.py:11
  272.2 45.4 %all-reduce.26.cloned.1.call-done = f32[1,512,256]{1,2,0:T(8,128)} async-done(((f32[1,512,256]{1,2,0:T(8,128)}), f32[1,512,256]{1,2,0:T(8,128)}) %all-reduce.26.cloned.1.call-update) | async-done | bytes 524304 | tf_op jit(solution)/shard_map/psum | solution.py:31
  323.4 35.5 %all-reduce.28.cloned.1.call-done = f32[512,256]{0,1:T(8,128)} async-done(((f32[512,256]{0,1:T(8,128)}), f32[512,256]{0,1:T(8,128)}) %all-reduce.28.cloned.1.call-update) | async-done | bytes 524304 | tf_op jit(solution)/shard_map/psum | solution.py:11
  362.1 55.0 %all-reduce.30.cloned.1.call-done = f32[512,256]{1,0:T(8,128)} async-done(((f32[512,256]{1,0:T(8,128)}), f32[512,256]{1,0:T(8,128)}) %all-reduce.30.cloned.1.call-update) | async-done | bytes 524304 | tf_op jit(solution)/shard_map/psum | solution.py:89
  419.3 38.5 %all-reduce.32.cloned.1.call-done = f32[512,256]{1,0:T(8,128)} async-done(((f32[512,256]{1,0:T(8,128)}), f32[512,256]{1,0:T(8,128)}) %all-reduce.32.cloned.1.call-update) | async-done | bytes 524304 | tf_op jit(solution)/shard_map/psum | solution.py:11
  461.6 45.4 %all-reduce.34.cloned.1.call-done = f32[512,256]{0,1:T(8,128)} async-done(((f32[512,256]{0,1:T(8,128)}), f32[512,256]{0,1:T(8,128)}) %all-reduce.34.cloned.1.call-update) | async-done | bytes 524304 | tf_op jit(solution)/shard_map/psum | solution.py:31
  510.0 38.4 %all-reduce.36.cloned.1.call-done = f32[1,512,256]{1,2,0:T(8,128)} async-done(((f32[1,512,256]{1,2,0:T(8,128)}), f32[1,512,256]{1,2,0:T(8,128)}) %all-reduce.36.cloned.1.call-update) | async-done | bytes 524304 | tf_op jit(solution)/shard_map/psum | solution.py:65
  551.3 13.0 %collective-permute-done = f32[1,512,256]{1,2,0:T(8,128)S(1)} collective-permute-done((f32[1,512,256]{1,2,0:T(8,128)}, f32[1,512,256]{1,2,0:T(8,128)S(1)}, u32[]{:S(2)}, u32[]{:S(2)}) %collective-permute-start) | collective-permute-done | bytes 524320 | tf_op jit(solution)/shard_map/ppermute | solution.py:50
  566.3 9.3 collective-permute-done.1
  575.7 9.0 collective-permute-done.2
  591.2 67.9 %all-reduce.38.cloned.1.call-done = f32[3,512,256]{1,2,0:T(8,128)} async-done(((f32[3,512,256]{1,2,0:T(8,128)}), f32[3,512,256]{1,2,0:T(8,128)}) %all-reduce.38.cloned.1.call-update) | async-done | bytes 1572880 | tf_op jit(solution)/shard_map/psum | solution.py:65
  662.1 35.6 %collective-permute-done.3 = f32[3,512,256]{1,2,0:T(8,128)} collective-permute-done((f32[3,512,256]{1,2,0:T(8,128)}, f32[3,512,256]{1,2,0:T(8,128)}, u32[]{:S(2)}, u32[]{:S(2)}) %collective-permute-start.3) | collective-permute-done | bytes 1572896 | tf_op jit(solution)/shard_map/ppermute | solution.py:50
  700.8 30.6 %collective-permute-done.4 = f32[3,512,256]{1,2,0:T(8,128)} collective-permute-done((f32[3,512,256]{1,2,0:T(8,128)}, f32[3,512,256]{1,2,0:T(8,128)}, u32[]{:S(2)}, u32[]{:S(2)}) %collective-permute-start.4) | collective-permute-done | bytes 1572896 | tf_op jit(solution)/shard_map/ppermute | solution.py:55
  732.9 29.8 %collective-permute-done.5 = f32[3,512,256]{1,2,0:T(8,128)} collective-permute-done((f32[3,512,256]{1,2,0:T(8,128)}, f32[3,512,256]{1,2,0:T(8,128)}, u32[]{:S(2)}, u32[]{:S(2)}) %collective-permute-start.5) | collective-permute-done | bytes 1572896 | tf_op jit(solution)/shard_map/ppermute | solution.py:50
  770.1 37.8 %all-reduce.40.cloned.1.call-done = f32[1,512,256]{1,2,0:T(8,128)} async-done(((f32[1,512,256]{1,2,0:T(8,128)}), f32[1,512,256]{1,2,0:T(8,128)}) %all-reduce.40.cloned.1.call-update) | async-done | bytes 524304 | tf_op jit(solution)/shard_map/psum | solution.py:65
  810.9 13.0 %collective-permute-done.6 = f32[1,512,256]{1,2,0:T(8,128)S(1)} collective-permute-done((f32[1,512,256]{1,2,0:T(8,128)}, f32[1,512,256]{1,2,0:T(8,128)S(1)}, u32[]{:S(2)}, u32[]{:S(2)}) %collective-permute-start.6) | collective-permute-done | bytes 524320 | tf_op jit(solution)/shard_map/ppermute | solution.py:50
  825.9 9.3 collective-permute-done.7
  835.2 9.0 collective-permute-done.8
  849.2 50.6 %all-reduce.42.cloned.1.call-done = f32[2,512,256]{1,2,0:T(8,128)} async-done(((f32[2,512,256]{1,2,0:T(8,128)}), f32[2,512,256]{1,2,0:T(8,128)}) %all-reduce.42.cloned.1.call-update) | async-done | bytes 1048592 | tf_op jit(solution)/shard_map/psum | solution.py:65
  902.8 24.2 %collective-permute-done.9 = f32[2,512,256]{1,2,0:T(8,128)S(1)} collective-permute-done((f32[2,512,256]{1,2,0:T(8,128)}, f32[2,512,256]{1,2,0:T(8,128)S(1)}, u32[]{:S(2)}, u32[]{:S(2)}) %collective-permute-start.9) | collective-permute-done | bytes 1048608 | tf_op jit(solution)/shard_map/ppermute | solution.py:50
  928.3 21.2 %collective-permute-done.10 = f32[2,512,256]{1,2,0:T(8,128)S(1)} collective-permute-done((f32[2,512,256]{1,2,0:T(8,128)}, f32[2,512,256]{1,2,0:T(8,128)S(1)}, u32[]{:S(2)}, u32[]{:S(2)}) %collective-permute-start.10) | collective-permute-done | bytes 1048608 | tf_op jit(solution)/shard_map/ppermute | solution.py:55
  949.6 21.5 %collective-permute-done.11 = f32[2,512,256]{1,2,0:T(8,128)S(1)} collective-permute-done((f32[2,512,256]{1,2,0:T(8,128)S(1)}, f32[2,512,256]{1,2,0:T(8,128)S(1)}, u32[]{:S(2)}, u32[]{:S(2)}) %collective-permute-start.11) | collective-permute-done | bytes 1048608 | tf_op jit(solution)/shard_map/ppermute | solution.py:50
  975.4 50.4 %all-reduce.44.cloned.1.call-done = f32[2,512,256]{1,2,0:T(8,128)} async-done(((f32[2,512,256]{1,2,0:T(8,128)}), f32[2,512,256]{1,2,0:T(8,128)}) %all-reduce.44.cloned.1.call-update) | async-done | bytes 1048592 | tf_op jit(solution)/shard_map/psum | solution.py:65
  1028.7 24.2 %collective-permute-done.12 = f32[2,512,256]{1,2,0:T(8,128)S(1)} collective-permute-done((f32[2,512,256]{1,2,0:T(8,128)}, f32[2,512,256]{1,2,0:T(8,128)S(1)}, u32[]{:S(2)}, u32[]{:S(2)}) %collective-permute-start.12) | collective-permute-done | bytes 1048608 | tf_op jit(solution)/shard_map/ppermute | solution.py:50
  1054.2 21.2 %collective-permute-done.13 = f32[2,512,256]{1,2,0:T(8,128)S(1)} collective-permute-done((f32[2,512,256]{1,2,0:T(8,128)}, f32[2,512,256]{1,2,0:T(8,128)S(1)}, u32[]{:S(2)}, u32[]{:S(2)}) %collective-permute-start.13) | collective-permute-done | bytes 1048608 | tf_op jit(solution)/shard_map/ppermute | solution.py:55
  1075.5 21.4 %collective-permute-done.14 = f32[2,512,256]{1,2,0:T(8,128)S(1)} collective-permute-done((f32[2,512,256]{1,2,0:T(8,128)S(1)}, f32[2,512,256]{1,2,0:T(8,128)S(1)}, u32[]{:S(2)}, u32[]{:S(2)}) %collective-permute-start.14) | collective-permute-done | bytes 1048608 | tf_op jit(solution)/shard_map/ppermute | solution.py:50
  (130 shorter events, 101.1 us)
Async XLA Ops:
  7.2 450.6 %copy-start = (f32[512,512]{1,0:T(8,128)S(1)}, f32[512,512]{1,0:T(8,128)}, u32[]{:S(2)}) copy-start(f32[512,512]{1,0:T(8,128)} %param.7) | copy-start | bytes 3145732
  7.2 58.3 %all-reduce.16.cloned.1.call-start = ((), (), s32[]{:S(2)}) async-start(), calls=%async_computation | async-start | bytes 2097152 | tf_op jit(solution)/shard_map/psum | solution.py:11
  10.1 112.4 %all-reduce.18.cloned.1.call-start = ((), (), s32[]{:S(2)}) async-start(), calls=%async_computation.1 | async-start | bytes 2097152 | tf_op jit(solution)/shard_map/psum | solution.py:31
  70.4 107.0 %all-reduce.20.cloned.1.call-start = ((), (), s32[]{:S(2)}) async-start(), calls=%async_computation.2 | async-start | bytes 2097152 | tf_op jit(solution)/shard_map/psum | solution.py:11
  124.8 102.2 %all-reduce.22.cloned.1.call-start = ((), (), s32[]{:S(2)}) async-start(), calls=%async_computation.3 | async-start | bytes 1048576 | tf_op jit(solution)/shard_map/psum | solution.py:31
  181.2 138.5 %copy-start.5 = (f32[2,512,256]{1,2,0:T(8,128)S(1)}, f32[2,512,256]{1,2,0:T(8,128)}, u32[]{:S(2)}) copy-start(f32[2,512,256]{1,2,0:T(8,128)} %all-reduce.20.cloned.1.call-done) | copy-start | bytes 3145732
  182.1 86.0 %all-reduce.24.cloned.1.call-start = ((), (), s32[]{:S(2)}) async-start(), calls=%async_computation.4 | async-start | bytes 1048576 | tf_op jit(solution)/shard_map/psum | solution.py:11
  229.1 88.6 %all-reduce.26.cloned.1.call-start = ((), (), s32[]{:S(2)}) async-start(), calls=%async_computation.5 | async-start | bytes 1048576 | tf_op jit(solution)/shard_map/psum | solution.py:31
  272.1 86.7 %all-reduce.28.cloned.1.call-start = ((), (), s32[]{:S(2)}) async-start(), calls=%async_computation.6 | async-start | bytes 1048576 | tf_op jit(solution)/shard_map/psum | solution.py:11
  319.5 97.6 %all-reduce.30.cloned.1.call-start = ((), (), s32[]{:S(2)}) async-start(), calls=%async_computation.7 | async-start | bytes 1048576 | tf_op jit(solution)/shard_map/psum | solution.py:89
  362.1 95.7 %all-reduce.32.cloned.1.call-start = ((), (), s32[]{:S(2)}) async-start(), calls=%async_computation.8 | async-start | bytes 1048576 | tf_op jit(solution)/shard_map/psum | solution.py:11
  419.2 87.8 %all-reduce.34.cloned.1.call-start = ((), (), s32[]{:S(2)}) async-start(), calls=%async_computation.9 | async-start | bytes 1048576 | tf_op jit(solution)/shard_map/psum | solution.py:31
  461.5 86.9 %all-reduce.36.cloned.1.call-start = ((), (), s32[]{:S(2)}) async-start(), calls=%async_computation.10 | async-start | bytes 1048576 | tf_op jit(solution)/shard_map/psum | solution.py:65
  509.9 149.2 %all-reduce.38.cloned.1.call-start = ((), (), s32[]{:S(2)}) async-start(), calls=%async_computation.11 | async-start | bytes 3145728 | tf_op jit(solution)/shard_map/psum | solution.py:65
  548.4 16.0 %collective-permute-start = (f32[1,512,256]{1,2,0:T(8,128)}, f32[1,512,256]{1,2,0:T(8,128)S(1)}, u32[]{:S(2)}, u32[]{:S(2)}) collective-permute-start(f32[1,512,256]{1,2,0:T(8,128)} %all-reduce.36.cloned.1.call-done), channel_id=1, source_target_pairs={{0,1},{1,2},{2,3},{3,0},{4,5},{5,6},{6,7},{7,4},{8,9},{9,10},{10,1... | collective-permute-start | bytes 1572872 | tf_op jit(solution)/shard_map/ppermute | solution.py:50
  549.9 25.8 %collective-permute-start.1 = (f32[1,512,256]{1,2,0:T(8,128)}, f32[1,512,256]{1,2,0:T(8,128)S(1)}, u32[]{:S(2)}, u32[]{:S(2)}) collective-permute-start(f32[1,512,256]{1,2,0:T(8,128)} %all-reduce.36.cloned.1.call-done), channel_id=1, source_target_pairs={{0,3},{1,0},{2,1},{3,2},{4,7},{5,4},{6,5},{7,6},{8,11},{9,8},{10,9... | collective-permute-start | bytes 1572872 | tf_op jit(solution)/shard_map/ppermute | solution.py:55
  564.4 20.3 %collective-permute-start.2 = (f32[1,512,256]{1,2,0:T(8,128)S(1)}, f32[1,512,256]{1,2,0:T(8,128)S(1)}, u32[]{:S(2)}, u32[]{:S(2)}) collective-permute-start(f32[1,512,256]{1,2,0:T(8,128)S(1)} %collective-permute-done), channel_id=1, source_target_pairs={{0,1},{1,2},{2,3},{3,0},{4,5},{5,6},{6,7},{7,4},{8,9},{9,10},{10,1... | collective-permute-start | bytes 1572872 | tf_op jit(solution)/shard_map/ppermute | solution.py:50
  591.2 216.8 %all-reduce.40.cloned.1.call-start = ((), (), s32[]{:S(2)}) async-start(), calls=%async_computation.12 | async-start | bytes 1048576 | tf_op jit(solution)/shard_map/psum | solution.py:65
  659.2 38.5 %collective-permute-start.3 = (f32[3,512,256]{1,2,0:T(8,128)}, f32[3,512,256]{1,2,0:T(8,128)}, u32[]{:S(2)}, u32[]{:S(2)}) collective-permute-start(f32[3,512,256]{1,2,0:T(8,128)} %all-reduce.38.cloned.1.call-done), channel_id=1, source_target_pairs={{0,1},{1,2},{2,3},{3,0},{4,5},{5,6},{6,7},{7,4},{8,9},{9,10},{10,1... | collective-permute-start | bytes 4718600 | tf_op jit(solution)/shard_map/ppermute | solution.py:50
  660.6 70.8 %collective-permute-start.4 = (f32[3,512,256]{1,2,0:T(8,128)}, f32[3,512,256]{1,2,0:T(8,128)}, u32[]{:S(2)}, u32[]{:S(2)}) collective-permute-start(f32[3,512,256]{1,2,0:T(8,128)} %all-reduce.38.cloned.1.call-done), channel_id=1, source_target_pairs={{0,3},{1,0},{2,1},{3,2},{4,7},{5,4},{6,5},{7,6},{8,11},{9,8},{10,9... | collective-permute-start | bytes 4718600 | tf_op jit(solution)/shard_map/ppermute | solution.py:55
  697.7 65.1 %collective-permute-start.5 = (f32[3,512,256]{1,2,0:T(8,128)}, f32[3,512,256]{1,2,0:T(8,128)}, u32[]{:S(2)}, u32[]{:S(2)}) collective-permute-start(f32[3,512,256]{1,2,0:T(8,128)} %collective-permute-done.3), channel_id=1, source_target_pairs={{0,1},{1,2},{2,3},{3,0},{4,5},{5,6},{6,7},{7,4},{8,9},{9,10},{10,1... | collective-permute-start | bytes 4718600 | tf_op jit(solution)/shard_map/ppermute | solution.py:50
  770.1 129.7 %all-reduce.42.cloned.1.call-start = ((), (), s32[]{:S(2)}) async-start(), calls=%async_computation.13 | async-start | bytes 2097152 | tf_op jit(solution)/shard_map/psum | solution.py:65
  808.0 16.0 %collective-permute-start.6 = (f32[1,512,256]{1,2,0:T(8,128)}, f32[1,512,256]{1,2,0:T(8,128)S(1)}, u32[]{:S(2)}, u32[]{:S(2)}) collective-permute-start(f32[1,512,256]{1,2,0:T(8,128)} %all-reduce.40.cloned.1.call-done), channel_id=1, source_target_pairs={{0,1},{1,2},{2,3},{3,0},{4,5},{5,6},{6,7},{7,4},{8,9},{9,10},{10,1... | collective-permute-start | bytes 1572872 | tf_op jit(solution)/shard_map/ppermute | solution.py:50
  809.4 25.8 %collective-permute-start.7 = (f32[1,512,256]{1,2,0:T(8,128)}, f32[1,512,256]{1,2,0:T(8,128)S(1)}, u32[]{:S(2)}, u32[]{:S(2)}) collective-permute-start(f32[1,512,256]{1,2,0:T(8,128)} %all-reduce.40.cloned.1.call-done), channel_id=1, source_target_pairs={{0,3},{1,0},{2,1},{3,2},{4,7},{5,4},{6,5},{7,6},{8,11},{9,8},{10,9... | collective-permute-start | bytes 1572872 | tf_op jit(solution)/shard_map/ppermute | solution.py:55
  823.9 20.3 %collective-permute-start.8 = (f32[1,512,256]{1,2,0:T(8,128)S(1)}, f32[1,512,256]{1,2,0:T(8,128)S(1)}, u32[]{:S(2)}, u32[]{:S(2)}) collective-permute-start(f32[1,512,256]{1,2,0:T(8,128)S(1)} %collective-permute-done.6), channel_id=1, source_target_pairs={{0,1},{1,2},{2,3},{3,0},{4,5},{5,6},{6,7},{7,4},{8,9},{9,10},{10,1... | collective-permute-start | bytes 1572872 | tf_op jit(solution)/shard_map/ppermute | solution.py:50
  849.2 176.6 %all-reduce.44.cloned.1.call-start = ((), (), s32[]{:S(2)}) async-start(), calls=%async_computation.14 | async-start | bytes 2097152 | tf_op jit(solution)/shard_map/psum | solution.py:65
  899.8 27.1 %collective-permute-start.9 = (f32[2,512,256]{1,2,0:T(8,128)}, f32[2,512,256]{1,2,0:T(8,128)S(1)}, u32[]{:S(2)}, u32[]{:S(2)}) collective-permute-start(f32[2,512,256]{1,2,0:T(8,128)} %all-reduce.42.cloned.1.call-done), channel_id=1, source_target_pairs={{0,1},{1,2},{2,3},{3,0},{4,5},{5,6},{6,7},{7,4},{8,9},{9,10},{10,1... | collective-permute-start | bytes 3145736 | tf_op jit(solution)/shard_map/ppermute | solution.py:50
  901.3 48.1 %collective-permute-start.10 = (f32[2,512,256]{1,2,0:T(8,128)}, f32[2,512,256]{1,2,0:T(8,128)S(1)}, u32[]{:S(2)}, u32[]{:S(2)}) collective-permute-start(f32[2,512,256]{1,2,0:T(8,128)} %all-reduce.42.cloned.1.call-done), channel_id=1, source_target_pairs={{0,3},{1,0},{2,1},{3,2},{4,7},{5,4},{6,5},{7,6},{8,11},{9,8},{10,9... | collective-permute-start | bytes 3145736 | tf_op jit(solution)/shard_map/ppermute | solution.py:55
  927.0 44.0 %collective-permute-start.11 = (f32[2,512,256]{1,2,0:T(8,128)S(1)}, f32[2,512,256]{1,2,0:T(8,128)S(1)}, u32[]{:S(2)}, u32[]{:S(2)}) collective-permute-start(f32[2,512,256]{1,2,0:T(8,128)S(1)} %collective-permute-done.9), channel_id=1, source_target_pairs={{0,1},{1,2},{2,3},{3,0},{4,5},{5,6},{6,7},{7,4},{8,9},{9,10},{10,1... | collective-permute-start | bytes 3145736 | tf_op jit(solution)/shard_map/ppermute | solution.py:50
  1025.8 27.1 %collective-permute-start.12 = (f32[2,512,256]{1,2,0:T(8,128)}, f32[2,512,256]{1,2,0:T(8,128)S(1)}, u32[]{:S(2)}, u32[]{:S(2)}) collective-permute-start(f32[2,512,256]{1,2,0:T(8,128)} %all-reduce.44.cloned.1.call-done), channel_id=1, source_target_pairs={{0,1},{1,2},{2,3},{3,0},{4,5},{5,6},{6,7},{7,4},{8,9},{9,10},{10,1... | collective-permute-start | bytes 3145736 | tf_op jit(solution)/shard_map/ppermute | solution.py:50
  1027.2 48.1 %collective-permute-start.13 = (f32[2,512,256]{1,2,0:T(8,128)}, f32[2,512,256]{1,2,0:T(8,128)S(1)}, u32[]{:S(2)}, u32[]{:S(2)}) collective-permute-start(f32[2,512,256]{1,2,0:T(8,128)} %all-reduce.44.cloned.1.call-done), channel_id=1, source_target_pairs={{0,3},{1,0},{2,1},{3,2},{4,7},{5,4},{6,5},{7,6},{8,11},{9,8},{10,9... | collective-permute-start | bytes 3145736 | tf_op jit(solution)/shard_map/ppermute | solution.py:55
  1052.9 44.0 %collective-permute-start.14 = (f32[2,512,256]{1,2,0:T(8,128)S(1)}, f32[2,512,256]{1,2,0:T(8,128)S(1)}, u32[]{:S(2)}, u32[]{:S(2)}) collective-permute-start(f32[2,512,256]{1,2,0:T(8,128)S(1)} %collective-permute-done.12), channel_id=1, source_target_pairs={{0,1},{1,2},{2,3},{3,0},{4,5},{5,6},{6,7},{7,4},{8,9},{9,10},{10,1... | collective-permute-start | bytes 3145736 | tf_op jit(solution)/shard_map/ppermute | solution.py:50
  (10 other events, 322.5 us)
Sparse Core Ops, SparseCore 0:
  11.0 54.5 all-reduce.15
  70.5 51.9 all-reduce.17
  125.5 51.8 all-reduce.19
  182.2 44.6 all-reduce.21
  229.7 38.2 all-reduce.23
  272.3 45.3 all-reduce.25
  320.6 38.2 all-reduce.27
  362.6 54.5 all-reduce.29
  420.2 37.5 all-reduce.31
  461.7 45.3 all-reduce.33
  510.1 38.2 all-reduce.35
  591.3 67.8 all-reduce.37
  770.2 37.6 all-reduce.39
  849.3 50.5 all-reduce.41
  975.5 50.2 all-reduce.43
